TPU v7x, 32 devices: a whole 2x2x4 slice. The times are simulated.
32 devices in a mesh: row: 8 (over z, y), col: 4 (over x, core).
Axes of the slice: x: 2, y: 2, z: 4, core: 2. Of those that a mesh axis runs over, the one named last changes fastest.
Arguments:
- tokens: bfloat16 [384, 8192], P('row', 'col'), may hold values from -6 to 6
- weight: bfloat16 [8192, 32768], P('col', 'row'), may hold values from -0.109375 to 0.109375
- tile_rows: int32 [8, 4, 256], P('row', 'col'), may hold values from 0 to 63, as said below
- tile_cols: int32 [8, 4, 256], P('row', 'col'), may hold values from 0 to 255, as said below
- tile_count: int32 [8, 4], P('row', 'col'), may hold values from 64 to 256, as said below
- hidden_cotangent: bfloat16 [384, 32768], P('col', 'row'), may hold values from -6 to 6
Outputs:
- hidden: bfloat16 [384, 32768], P('col', 'row')
- input_grad: bfloat16 [384, 8192], P('row', 'col')
- weight_grad: bfloat16 [8192, 32768], P('col', 'row')
Inputs may be any that keep to these rules, and one draw needn't show every extreme that they name: tile_rows[r, c, k] is a row block of the weight (tiles of 128 x 128) among the 16 blocks from c * 16 on, which index c of col holds. tile_cols[r, c, k] is a column block among the 32 blocks from r * 32 on, which index r of row holds; the 256 candidate tiles of one device are distinct. The first tile_count[r, c] candidates of device (r, c) are its nonzero tiles; some device holds 256.
All inputs are finite; a program needn't handle non-finite values.
Results may differ from a plain program's by a relative error of at most 0.0049.
Values may be sent and summed in bfloat16 or wider, within the bound.
A program may use at most 128 MiB of HBM per device.

v0:
```python
import jax
import jax.numpy as jnp
from jax import lax
from jax.experimental import pallas as pl
from jax.experimental.pallas import tpu as pltpu
from jax.sharding import PartitionSpec as P

TILE = 128


def exchange_sum(partial, axis):
    n = lax.psum(1, axis)
    rows = partial.shape[0] // n
    mine = lax.all_to_all(
        partial.reshape(n, rows, partial.shape[1]), axis, split_axis=0, concat_axis=0
    )
    return mine.astype(jnp.float32).sum(axis=0)


def paired_exchange_sum(partial, axis):
    n = lax.psum(1, axis)
    if n % 2:
        return exchange_sum(partial, axis)
    chips = n // 2
    rows = partial.shape[0] // n
    here = lax.axis_index(axis)
    chip, core = here // 2, here % 2
    blocks = partial.reshape(chips, 2, rows, partial.shape[1])
    away = lax.dynamic_index_in_dim(blocks, 1 - core, 1, keepdims=False)
    keep = lax.dynamic_index_in_dim(blocks, core, 1, keepdims=False)
    came = lax.ppermute(away, axis, [(i, i ^ 1) for i in range(n)])

    def pair_block(which):
        ours = lax.dynamic_index_in_dim(keep, which, 0, keepdims=False)
        theirs = lax.dynamic_index_in_dim(came, which, 0, keepdims=False)
        return ours.astype(jnp.float32) + theirs.astype(jnp.float32)

    arrived = [
        lax.ppermute(
            pair_block((chip + step) % chips).astype(jnp.bfloat16),
            axis,
            [(i, (i + 2 * step) % n) for i in range(n)],
        )
        for step in range(1, chips)
    ]
    total = pair_block(chip)
    for block in arrived:
        total = total + block.astype(jnp.float32)
    return total


def mask_weight(mask_ref, weight_ref, held):
    for block in range(mask_ref.shape[0]):
        rows = pl.ds(block * TILE, TILE)
        tile = weight_ref[rows, :]
        live = jnp.broadcast_to(mask_ref[block : block + 1, :], tile.shape) > 0.5
        held[rows, :] = jnp.where(live, tile.astype(jnp.float32), 0.0).astype(jnp.bfloat16)


def forward_kernel(mask_ref, tokens_ref, weight_ref, out_ref, held):
    mask_weight(mask_ref, weight_ref, held)
    out_ref[...] = jnp.dot(
        tokens_ref[...], held[...], preferred_element_type=jnp.float32
    ).astype(jnp.bfloat16)


def backward_kernel(mask_ref, grads_ref, weight_ref, out_ref, held, total):
    step = pl.program_id(0)
    mask_weight(mask_ref, weight_ref, held)
    product = lax.dot_general(
        grads_ref[...], held[...], (((1,), (1,)), ((), ())), preferred_element_type=jnp.float32
    )

    @pl.when(step == 0)
    def _():
        total[...] = product

    @pl.when(step > 0)
    def _():
        total[...] += product

    @pl.when(step == pl.num_programs(0) - 1)
    def _():
        out_ref[...] = total[...].astype(jnp.bfloat16)


def weight_kernel(mask_ref, turned_ref, grads_ref, out_ref):
    for block in range(mask_ref.shape[0]):
        rows = pl.ds(block * TILE, TILE)
        product = jnp.dot(
            turned_ref[rows, :], grads_ref[...], preferred_element_type=jnp.float32
        )
        live = jnp.broadcast_to(mask_ref[block : block + 1, :], product.shape) > 0.5
        out_ref[rows, :] = jnp.where(live, product, 0.0).astype(jnp.bfloat16)


def run(kernel, mask, left, right, width, left_blocked, out, out_blocked, scratch):
    blocks, total_width = mask.shape
    depth = blocks * TILE
    column = lambda rows: pl.BlockSpec((rows, width), lambda i: (0, i))
    whole = lambda shape: pl.BlockSpec(shape, lambda i: (0, 0))
    moved = sum(a.size * a.dtype.itemsize for a in (left, right)) + out[0] * out[1] * 2
    count = left.shape[1] if kernel is weight_kernel else left.shape[0]
    return pl.pallas_call(
        kernel,
        grid=(total_width // width,),
        in_specs=[
            column(blocks),
            column(left.shape[0]) if left_blocked else whole(left.shape),
            column(right.shape[0]),
        ],
        out_specs=column(out[0]) if out_blocked else whole(out),
        out_shape=jax.ShapeDtypeStruct(out, jnp.bfloat16),
        scratch_shapes=scratch,
        cost_estimate=pl.CostEstimate(
            flops=2 * count * depth * total_width, bytes_accessed=moved, transcendentals=0
        ),
        compiler_params=pltpu.CompilerParams(
            dimension_semantics=("arbitrary",), vmem_limit_bytes=48 * 1024 * 1024
        ),
    )(mask, left, right)


def on_device(tokens, weight, tile_rows, tile_cols, tile_count, hidden_cotangent):
    row_index = lax.axis_index("row")
    col_index = lax.axis_index("col")
    row_blocks = weight.shape[0] // TILE
    col_blocks = weight.shape[1] // TILE
    capacity = tile_rows.shape[2]
    local_rows = tile_rows.reshape(capacity) - col_index * row_blocks
    local_cols = tile_cols.reshape(capacity) - row_index * col_blocks
    is_live = jnp.arange(capacity) < tile_count.reshape(())
    row_pick = (
        (local_rows[None, :] == jnp.arange(row_blocks)[:, None]) & is_live[None, :]
    ).astype(jnp.bfloat16)
    col_pick = (local_cols[:, None] == (jnp.arange(weight.shape[1]) // TILE)[None, :]).astype(
        jnp.bfloat16
    )
    mask = jnp.dot(row_pick, col_pick, preferred_element_type=jnp.float32)
    width = min(512, weight.shape[1])
    held = pltpu.VMEM((weight.shape[0], width), jnp.bfloat16)

    full_tokens = lax.all_gather(tokens, "row", axis=0, tiled=True)
    count = full_tokens.shape[0]
    partial = run(
        forward_kernel, mask, full_tokens, weight, width, False,
        (count, weight.shape[1]), True, [held],
    )
    pre_act = paired_exchange_sum(partial, "col")
    gate_value = jax.nn.sigmoid(pre_act)
    hidden = (pre_act * gate_value).astype(jnp.bfloat16)
    silu_slope = gate_value * (1.0 + pre_act * (1.0 - gate_value))
    grad_pre = (hidden_cotangent.astype(jnp.float32) * silu_slope).astype(jnp.bfloat16)
    full_grads = lax.all_gather(grad_pre, "col", axis=0, tiled=True)
    share_shape = (count, weight.shape[0])
    share = run(
        backward_kernel, mask, full_grads, weight, width, True,
        share_shape, False, [held, pltpu.VMEM(share_shape, jnp.float32)],
    )
    input_grad = exchange_sum(share, "row").astype(jnp.bfloat16)
    weight_grad = run(
        weight_kernel, mask, full_tokens.T, full_grads, width, False,
        weight.shape, True, [],
    )
    return (hidden, input_grad, weight_grad)


def solution(mesh):
    in_specs = (
        P("row", "col"),
        P("col", "row"),
        P("row", "col", None),
        P("row", "col", None),
        P("row", "col"),
        P("col", "row"),
    )
    out_specs = (P("col", "row"), P("row", "col"), P("col", "row"))
    return jax.shard_map(
        on_device, mesh=mesh, in_specs=in_specs, out_specs=out_specs, check_vma=False
    )
```

profile of v0, /device:TPU:0, one launch (start us, length us, event | category | flops | bytes accessed | tf_op | source)
XLA Modules:
  0.0 196.8 jit_solution(5473653634758635045)
XLA Ops:
  7.2 0.0 all-gather.3.cloned.1.call-start
  7.2 0.7 all-gather.3.cloned.1.call-update
  7.9 0.0 all-gather.5.cloned.1.call-start
  8.6 0.7 broadcast_subtract_fusion.1
  9.3 0.7 broadcast_subtract_fusion
  10.0 0.8 fusion.mask_ref
  10.8 46.3 %all-gather.3.cloned.1.call-done.tokens_ref = bf16[384,2048]{1,0:T(8,128)(2,1)} async-done(((bf16[48,2048]{1,0:T(8,128)(2,1)}), bf16[384,2048]{1,0:T(8,128)(2,1)}) %all-gather.3.cloned.1.call-update) | async-done | bytes 1572880 | tf_op jit(solution)/shard_map/all_gather | solution.py:143
  57.1 0.0 copy-start
  57.1 1.4 copy-done
  58.5 11.8 %shard_map.85 = bf16[384,4096]{1,0:T(8,128)(2,1)S(1)} custom-call(f32[16,4096]{1,0:T(8,128)S(1)} %fusion.mask_ref, bf16[384,2048]{1,0:T(8,128)(2,1)S(1)} %copy-done, bf16[2048,4096]{1,0:T(8,128)(2,1)} %weight_ref.3), custom_call_target="tpu_custom_call" | custom-call | flops 6442450944 | bytes 21495808 | tf_op jit(solution)/shard_map/pallas_call | solution.py:104
  70.3 1.3 dynamic-slice_bitcast_fusion
  71.5 0.0 collective-permute-start
  71.5 3.7 %collective-permute-done = bf16[2,96,4096]{2,1,0:T(8,128)(2,1)} collective-permute-done((bf16[2,96,4096]{2,1,0:T(8,128)(2,1)}, bf16[2,96,4096]{2,1,0:T(8,128)(2,1)}, u32[]{:S(2)}, u32[]{:S(2)}) %collective-permute-start) | collective-permute-done | bytes 1572896 | tf_op jit(solution)/shard_map/ppermute | solution.py:31
  75.3 2.2 %fusion.4 = bf16[96,4096]{1,0:T(8,128)(2,1)} fusion(bf16[2,96,4096]{2,1,0:T(8,128)(2,1)} %collective-permute-done, s32[]{:T(128)S(6)} %select_n.55, bf16[2,2,96,4096]{3,2,1,0:T(8,128)(2,1)S(1)} %bitcast.24, s32[]{:T(128)S(6)} %select_n.56, s32[]{:T(128)S(6)} %select_n.52), kind=kLoop, calls=%fused_computation.5 | loop fusion | flops 1572864 | bytes 2359308 | tf_op jit(solution)/shard_map/convert_element_type | solution.py:40
  77.5 1.5 collective-permute-start.1
  78.9 18.4 %collective-permute-done.1 = bf16[96,4096]{1,0:T(8,128)(2,1)} collective-permute-done((bf16[96,4096]{1,0:T(8,128)(2,1)}, bf16[96,4096]{1,0:T(8,128)(2,1)}, u32[]{:S(2)}, u32[]{:S(2)}) %collective-permute-start.1) | collective-permute-done | bytes 786464 | tf_op jit(solution)/shard_map/ppermute | solution.py:39
  97.4 3.6 %multiply_convert_fusion = (bf16[96,4096]{1,0:T(8,128)(2,1)}, bf16[96,4096]{1,0:T(8,128)(2,1)}) fusion(bf16[96,4096]{1,0:T(8,128)(2,1)} %param.11, bf16[96,4096]{1,0:T(8,128)(2,1)} %collective-permute-done.1, bf16[2,96,4096]{2,1,0:T(8,128)(2,1)} %collective-permute-done, s32[]{:T(128)S(6)} %select_n.48, bf16[2,2,96,4096]{3,2,1,0:T(8,128)(2,1)S(1)} %bitcast.25, ...), kind=kLoop, calls=%fused_computation.8 | loop fusion | flops 6684672 | bytes 4718604 | tf_op jit(solution)/shard_map/convert_element_type | solution.py:153
  101.0 0.0 all-gather.5.cloned.1.call-update
  101.0 27.0 %all-gather.5.cloned.1.call-done.grads_ref = bf16[384,4096]{1,0:T(8,128)(2,1)} async-done(((bf16[96,4096]{1,0:T(8,128)(2,1)}), bf16[384,4096]{1,0:T(8,128)(2,1)}) %all-gather.5.cloned.1.call-update) | async-done | bytes 3145744 | tf_op jit(solution)/shard_map/all_gather | solution.py:154
  128.0 0.0 copy-start.2
  128.0 1.9 copy-done.2
  129.9 14.5 %shard_map.86 = bf16[384,2048]{1,0:T(8,128)(2,1)} custom-call(f32[16,4096]{1,0:T(8,128)S(1)} %fusion.mask_ref, bf16[384,4096]{1,0:T(8,128)(2,1)S(1)} %copy-done.2, bf16[2048,4096]{1,0:T(8,128)(2,1)} %weight_ref.3), custom_call_target="tpu_custom_call" | custom-call | flops 6442450944 | bytes 21495808 | tf_op jit(solution)/shard_map/pallas_call | solution.py:104
  144.4 0.0 copy-start.1
  144.4 5.6 %all-to-all-start = ((bf16[8,48,2048]{2,1,0:T(8,128)(2,1)}), bf16[8,48,2048]{2,1,0:T(8,128)(2,1)}, u32[]{:S(2)}, u32[]{:S(2)}) async-start(bf16[8,48,2048]{2,1,0:T(8,128)(2,1)} %bitcast.9), calls=%async_computation | async-start | bytes 3145728 | tf_op jit(solution)/shard_map/all_to_all | solution.py:14
  150.0 0.0 copy-done.1
  150.0 0.9 copy.11
  150.9 0.0 copy-start.3
  150.9 1.9 copy-done.3
  152.8 11.8 %shard_map.87 = bf16[2048,4096]{1,0:T(8,128)(2,1)} custom-call(f32[16,4096]{1,0:T(8,128)S(1)} %fusion.mask_ref, bf16[2048,384]{1,0:T(8,128)(2,1)S(1)} %bitcast.26, bf16[384,4096]{1,0:T(8,128)(2,1)S(1)} %copy-done.3), custom_call_target="tpu_custom_call" | custom-call | flops 6442450944 | bytes 21495808 | tf_op jit(solution)/shard_map/pallas_call | solution.py:104
  164.6 23.0 %all-to-all-done = bf16[8,48,2048]{2,1,0:T(8,128)(2,1)} async-done(((bf16[8,48,2048]{2,1,0:T(8,128)(2,1)}), bf16[8,48,2048]{2,1,0:T(8,128)(2,1)}, u32[]{:S(2)}, u32[]{:S(2)}) %all-to-all-start) | async-done | bytes 1572896 | tf_op jit(solution)/shard_map/all_to_all | solution.py:14
  187.5 2.4 %reduce_sum.12 = bf16[48,2048]{1,0:T(8,128)(2,1)} reduce(bf16[8,48,2048]{2,1,0:T(8,128)(2,1)} %all-to-all-done, bf16[]{:T(256)} %constant.119.clone.1), dimensions={0}, to_apply=%region_0.1 | reduce | flops 688128 | bytes 1769474 | tf_op jit(solution)/shard_map/reduce_sum | solution.py:17
  (2 shorter events, 0.0 us)
Async XLA Ops:
  7.2 49.9 %all-gather.3.cloned.1.call-start = ((), (), s32[]{:S(2)}) async-start(), calls=%async_computation.1 | async-start | bytes 1769472 | tf_op jit(solution)/shard_map/all_gather | solution.py:143
  7.9 120.1 %all-gather.5.cloned.1.call-start = ((), (), s32[]{:S(2)}) async-start(), calls=%async_computation.2 | async-start | bytes 3932160 | tf_op jit(solution)/shard_map/all_gather | solution.py:154
  57.1 1.4 copy-start
  71.5 3.8 %collective-permute-start = (bf16[2,96,4096]{2,1,0:T(8,128)(2,1)}, bf16[2,96,4096]{2,1,0:T(8,128)(2,1)}, u32[]{:S(2)}, u32[]{:S(2)}) collective-permute-start(bf16[2,96,4096]{2,1,0:T(8,128)(2,1)} %dynamic-slice_bitcast_fusion), channel_id=1, source_target_pairs={{0,1},{1,0},{2,3},{3,2},{4,5},{5,4},{6,7},{7,6},{8,9},{9,8},{10,11... | collective-permute-start | bytes 4718600 | tf_op jit(solution)/shard_map/ppermute | solution.py:31
  77.5 19.9 %collective-permute-start.1 = (bf16[96,4096]{1,0:T(8,128)(2,1)}, bf16[96,4096]{1,0:T(8,128)(2,1)}, u32[]{:S(2)}, u32[]{:S(2)}) collective-permute-start(bf16[96,4096]{1,0:T(8,128)(2,1)} %fusion.4), channel_id=1, source_target_pairs={{0,2},{1,3},{2,0},{3,1},{4,6},{5,7},{6,4},{7,5},{8,10},{9,11},{10,... | collective-permute-start | bytes 2359304 | tf_op jit(solution)/shard_map/ppermute | solution.py:39
  128.0 1.9 copy-start.2
  144.4 5.7 %copy-start.1 = (bf16[384,2048]{1,0:T(8,128)(2,1)S(1)}, bf16[384,2048]{1,0:T(8,128)(2,1)}, u32[]{:S(2)}) copy-start(bf16[384,2048]{1,0:T(8,128)(2,1)} %all-gather.3.cloned.1.call-done.tokens_ref) | copy-start | bytes 4718596
  144.4 43.2 %all-to-all-start = ((bf16[8,48,2048]{2,1,0:T(8,128)(2,1)}), bf16[8,48,2048]{2,1,0:T(8,128)(2,1)}, u32[]{:S(2)}, u32[]{:S(2)}) async-start(bf16[8,48,2048]{2,1,0:T(8,128)(2,1)} %bitcast.9), calls=%async_computation | async-start | bytes 3145728 | tf_op jit(solution)/shard_map/all_to_all | solution.py:14
  150.9 1.9 copy-start.3
Sparse Core Ops, SparseCore 0:
  10.2 46.8 all-gather.2
  101.1 26.8 all-gather.4
where the time goes:
time: 197 us
  waiting for transfers between devices  119 us (60%)
  Pallas kernels  38 us (19%)
  between operations  14.8 us (8%)
  other arithmetic  9.56 us (5%)
  local copies, waits for them, and re-layouts  7.3 us (4%)
  starting transfers between devices  7.19 us (4%)
    all_gather x1, waiting for transfers between devices, on_device(): full_tokens = lax.all_gather(tokens, 'row', axis=0, tiled=True)  46.3 us
    pallas_call x3, Pallas kernels, run(): pl.pallas_call(kernel, grid=(total_width // width,), in_specs=[column(blo...  38 us
    all_gather x1, waiting for transfers between devices, on_device(): full_grads = lax.all_gather(grad_pre, 'col', axis=0, tiled=True)  27 us
    all_to_all x1, waiting for transfers between devices, exchange_sum(): lax.all_to_all(partial.reshape(n, rows, partial.shape[1]), axis, split_ax...  23 us
    ppermute x1, waiting for transfers between devices, paired_exchange_sum(): lax.ppermute(pair_block((chip + step) % chips).astype(jnp.bfloat16), axis...  18.4 us
    all_to_all x1, starting transfers between devices, exchange_sum(): lax.all_to_all(partial.reshape(n, rows, partial.shape[1]), axis, split_ax...  5.65 us
    unnamed x8, local copies, waits for them, and re-layouts  5.18 us
  transfers between devices with their start and end apart: 5, of which 5 were waited for; matrix products, arithmetic and copies ran while one was open for 2% of the time, Pallas kernels for 6%

commit v1 on v0

v1 whole, which is shorter than its diff:
```python
import functools

import jax
import jax.numpy as jnp
from jax import lax
from jax.experimental import pallas as pl
from jax.experimental.pallas import tpu as pltpu
from jax.sharding import PartitionSpec as P

TILE = 128
SUB = 16
LAG_SUM = 2
LAG_PASS = 4
LAG_BACK = 5
MESH = pl.DeviceIdType.MESH
F32 = jnp.float32
BF16 = jnp.bfloat16


class Plan:
    def __init__(self, n_row, n_col, tokens, weight):
        self.n_row, self.n_col = n_row, n_col
        self.block, self.depth = tokens.shape
        self.wide = weight.shape[1]
        self.line = n_row // 2
        self.chips = n_col // 2
        self.per_owner = n_row // n_col
        self.groups = self.block // SUB
        self.rows = n_row * SUB
        self.slab = self.per_owner * SUB
        self.chunks = 4
        self.cut = self.wide // self.chunks
        self.units = self.groups * self.chunks
        self.halves = 2
        self.part = self.depth // self.halves
        self.step = min(256, self.cut)
        self.row_blocks = self.depth // TILE
        self.col_blocks = self.wide // TILE


def comm_kernel(
    p,
    tokens, weight, tile_rows, tile_cols, count, cot,
    hidden, ingrad, turned_out, grads_out, mask_out,
    w, mask, toks, turned, grads, share, c1s, c1r, keep, c2s, c2r, own, hid, cotv,
    r1s, r1r, rkeep, r2s, r2r, rown, inout,
    w_sem, local_sem, hid_sem,
    ag_send, ag_fwd, ag_recv, c1_send, c1_recv, c2_send, c2_recv, c3_send, c3_recv,
    c4_send, c4_recv, r1_send, r1_recv, r2_send, r2_recv,
):
    row, col = lax.axis_index("row"), lax.axis_index("col")
    pair, line = lax.rem(row, 2), lax.div(row, 2)
    core, chip = lax.rem(col, 2), lax.div(col, 2)
    partner = (line * 2 + 1 - pair, col)
    sibling = (row, chip * 2 + 1 - core)

    def line_peer(step):
        return lax.rem(line + step, p.line)

    def chip_peer(step):
        return lax.rem(chip + step, p.chips)

    def place(block):
        owner = lax.div(block, p.per_owner)
        other = lax.rem(lax.rem(owner, 2) + core, 2)
        slab = other * p.chips + lax.div(owner, 2)
        return pl.multiple_of(slab * p.slab + lax.rem(block, p.per_owner) * SUB, SUB)

    def remote(src, dst, send, recv, device):
        return pltpu.make_async_remote_copy(
            src_ref=src, dst_ref=dst, send_sem=send, recv_sem=recv,
            device_id=device, device_id_type=MESH,
        )

    def load_weight(j):
        return pltpu.make_async_copy(
            weight.at[:, pl.ds(j * p.cut, p.cut)], w.at[j], w_sem.at[j]
        )

    def own_rows(g):
        return tokens.at[pl.ds(pl.multiple_of(g * SUB, SUB), SUB), :]

    def tok_rows(g, block):
        return toks.at[g, pl.ds(place(block), SUB), :]

    def load_own(g):
        return pltpu.make_async_copy(own_rows(g), tok_rows(g, row), local_sem.at[g])

    def ag_line(g, step):
        return remote(
            own_rows(g), tok_rows(g, row), ag_send.at[g, step], ag_recv.at[g, row],
            (line_peer(step) * 2 + pair, col),
        )

    def ag_pair(g):
        return remote(
            own_rows(g), tok_rows(g, row), ag_send.at[g, 0], ag_recv.at[g, row], partner
        )

    def ag_pass(g, step):
        block = line_peer(step) * 2 + pair
        return remote(
            tok_rows(g, block), tok_rows(g, block), ag_fwd.at[g, step], ag_recv.at[g, block],
            partner,
        )

    def ag_arrival(g, block):
        return remote(
            tok_rows(g, block), tok_rows(g, block), ag_send.at[g, 0], ag_recv.at[g, block],
            partner,
        )

    def slab_rows(j, g, index):
        start = pl.multiple_of(g * p.rows + index * p.slab, SUB)
        return grads.at[j, pl.ds(start, p.slab), :]

    def c1_copy(u):
        return remote(c1s.at[u], c1r.at[u], c1_send.at[u], c1_recv.at[u], sibling)

    def c2_copy(u, step):
        return remote(
            c2s.at[u, step], c2r.at[u, step], c2_send.at[u, step], c2_recv.at[u, step],
            (row, chip_peer(step) * 2 + core),
        )

    def c3_copy(u, g, j, step):
        return remote(
            slab_rows(j, g, chip), slab_rows(j, g, chip), c3_send.at[u, step],
            c3_recv.at[u, step], (row, chip_peer(step) * 2 + core),
        )

    def c3_arrival(u, g, j, step):
        source = lax.rem(chip + p.chips - step, p.chips)
        return remote(
            slab_rows(j, g, source), slab_rows(j, g, source), c3_send.at[u, step],
            c3_recv.at[u, step], (row, source * 2 + core),
        )

    def c4_copy(u, g, j, step):
        source = lax.rem(chip + p.chips - step, p.chips)
        return remote(
            slab_rows(j, g, source), slab_rows(j, g, p.chips + source), c4_send.at[u, step],
            c4_recv.at[u, step], sibling,
        )

    def hid_copy(u, g, j, i):
        start = pl.multiple_of(i * p.block + g * SUB, SUB)
        return pltpu.make_async_copy(
            hid.at[u, pl.ds(i * SUB, SUB), :],
            hidden.at[pl.ds(start, SUB), pl.ds(pl.multiple_of(j * p.cut, 128), p.cut)],
            hid_sem.at[u, i],
        )

    def r1_copy(g, h):
        return remote(
            r1s.at[g, h], r1r.at[g, h], r1_send.at[g, h], r1_recv.at[g, h], partner
        )

    def r2_copy(g, h, step):
        return remote(
            r2s.at[g, h, step], r2r.at[g, h, step], r2_send.at[g, h, step],
            r2_recv.at[g, h, step], (line_peer(step) * 2 + pair, col),
        )

    def gather_start(g):
        for step in range(1, p.line):
            ag_line(g, step).start()
        ag_pair(g).start()

    def gather_pass(g):
        for step in range(1, p.line):
            block = line_peer(step) * 2 + pair
            ag_arrival(g, block).wait_recv()
            ag_pass(g, step).start()

    def gather_rest(g):
        for step in range(p.line):
            ag_arrival(g, line_peer(step) * 2 + 1 - pair).wait_recv()

    def mask_chunk(j):
        load_weight(j).wait()
        for block in range(p.row_blocks):
            rows = pl.ds(block * TILE, TILE)
            one = mask[j, pl.ds(block * SUB, SUB), :]
            w[j, rows, :] = w[j, rows, :] * jnp.concatenate([one] * (TILE // SUB), axis=0)

    def forward(u, g, j):
        half = p.rows // 2
        for n in range(p.cut // p.step):
            cols = pl.ds(n * p.step, p.step)
            product = jnp.dot(toks[g], w[j, :, cols], preferred_element_type=F32)
            keep[:, cols] = product[:half]
            c1s[u, :, cols] = product[half:].astype(BF16)
        c1_copy(u).start()

    def pair_sum(u):
        c1_copy(u).wait_recv()
        for step in range(1, p.chips):
            rows = pl.ds(pl.multiple_of(chip_peer(step) * p.slab, SUB), p.slab)
            c2s[u, step] = (keep[rows, :] + c1r[u, rows, :].astype(F32)).astype(BF16)
            c2_copy(u, step).start()
        rows = pl.ds(pl.multiple_of(chip * p.slab, SUB), p.slab)
        own[lax.rem(u, LAG_SUM + 1)] = keep[rows, :] + c1r[u, rows, :].astype(F32)

    def activate(u, g, j):
        for step in range(1, p.chips):
            c2_copy(u, step).wait_recv()
        cols = pl.ds(pl.multiple_of(j * p.cut, 128), p.cut)
        for i in range(p.per_owner):
            rows = pl.ds(i * SUB, SUB)
            pre = own[lax.rem(u, LAG_SUM + 1), rows, :]
            for step in range(1, p.chips):
                pre = pre + c2r[u, step, rows, :].astype(F32)
            gate = jax.nn.sigmoid(pre)
            hid[u, rows, :] = (pre * gate).astype(BF16)
            slope = gate * (1.0 + pre * (1.0 - gate))
            start = pl.multiple_of(i * p.block + g * SUB, SUB)
            back = cotv[pl.ds(start, SUB), cols].astype(F32) * slope
            spot = pl.multiple_of(g * p.rows + chip * p.slab + i * SUB, SUB)
            grads[j, pl.ds(spot, SUB), :] = back.astype(BF16)
        for step in range(1, p.chips):
            c3_copy(u, g, j, step).start()
        c4_copy(u, g, j, 0).start()
        for i in range(p.per_owner):
            hid_copy(u, g, j, i).start()

    def hand_on(u, g, j):
        for step in range(1, p.chips):
            c3_arrival(u, g, j, step).wait_recv()
            c4_copy(u, g, j, step).start()

    def backward(u, g, j):
        for step in range(p.chips):
            c4_copy(u, g, j, step).wait_recv()
        first = (j == 0).astype(F32)
        left = grads[j, pl.ds(pl.multiple_of(g * p.rows, SUB), p.rows), :]
        for h in range(p.halves):
            for n in range(p.part // p.step):
                cols = pl.ds(h * p.part + n * p.step, p.step)
                product = lax.dot_general(
                    left, w[j, cols, :], (((1,), (1,)), ((), ())), preferred_element_type=F32
                )
                share[:, cols] = jnp.where(first > 0.5, 0.0, share[:, cols]) + product

            @pl.when(j == p.chunks - 1)
            def _():
                cols = pl.ds(h * p.part, p.part)
                for k in range(p.line):
                    away = share[pl.ds(place(2 * k + 1 - pair), SUB), cols]
                    r1s[g, h, k * SUB : (k + 1) * SUB, :] = away.astype(BF16)
                r1_copy(g, h).start()
                for k in range(p.line):
                    stay = share[pl.ds(place(2 * k + pair), SUB), cols]
                    rkeep[g, h, k * SUB : (k + 1) * SUB, :] = stay

    def reduce_pair(g, h):
        r1_copy(g, h).wait_recv()
        for step in range(1, p.line):
            rows = pl.ds(pl.multiple_of(line_peer(step) * SUB, SUB), SUB)
            both = rkeep[g, h, rows, :] + r1r[g, h, rows, :].astype(F32)
            r2s[g, h, step] = both.astype(BF16)
            r2_copy(g, h, step).start()
        rows = pl.ds(pl.multiple_of(line * SUB, SUB), SUB)
        rown[g, h] = rkeep[g, h, rows, :] + r1r[g, h, rows, :].astype(F32)

    def reduce_line(g, h):
        total = rown[g, h]
        for step in range(1, p.line):
            r2_copy(g, h, step).wait_recv()
            total = total + r2r[g, h, step].astype(F32)
        inout[g * SUB : (g + 1) * SUB, h * p.part : (h + 1) * p.part] = total.astype(BF16)

    for j in range(p.chunks):
        load_weight(j).start()
    load_cot = pltpu.make_async_copy(cot, cotv, local_sem.at[p.groups])
    for g in range(p.groups):
        load_own(g).start()
    load_cot.start()

    barrier = pltpu.get_barrier_semaphore()
    peers = [partner, sibling]
    peers += [(line_peer(s) * 2 + pair, col) for s in range(1, p.line)]
    peers += [(row, chip_peer(s) * 2 + core) for s in range(1, p.chips)]
    for peer in peers:
        pl.semaphore_signal(barrier, inc=1, device_id=peer, device_id_type=MESH)
    pl.semaphore_wait(barrier, len(peers))
    gather_start(0)

    cap = tile_rows.shape[2]
    local_rows = tile_rows[0] - col * p.row_blocks
    local_cols = tile_cols[0] - row * p.col_blocks
    live = lax.broadcasted_iota(jnp.int32, (1, cap), 1) < count[0, 0]
    local_rows = jnp.where(live, local_rows, -1)
    row_of = lax.broadcasted_iota(jnp.int32, (p.row_blocks * SUB, cap), 0) // SUB
    row_pick = (row_of == local_rows).astype(F32)
    col_of = lax.broadcasted_iota(jnp.int32, (p.col_blocks, cap), 0)
    col_pick = (col_of == local_cols).astype(F32)
    blocks = lax.dot_general(
        row_pick, col_pick, (((1,), (1,)), ((), ())), preferred_element_type=F32
    )
    for j in range(p.chunks):
        lane_of = lax.broadcasted_iota(jnp.int32, (p.col_blocks, p.cut), 1) + j * p.cut
        block_of = lax.broadcasted_iota(jnp.int32, (p.col_blocks, p.cut), 0)
        spread = (lane_of // TILE == block_of).astype(F32)
        mask[j] = jnp.dot(blocks, spread, preferred_element_type=F32).astype(BF16)
    save_mask = pltpu.make_async_copy(mask, mask_out, local_sem.at[p.groups + 1])
    save_mask.start()
    early = p.chunks // 2
    for j in range(early):
        mask_chunk(j)
    gather_pass(0)
    for g in range(1, p.groups):
        gather_start(g)
    for j in range(early, p.chunks):
        mask_chunk(j)
    for g in range(p.groups):
        load_own(g).wait()
    load_cot.wait()

    def place_of(u):
        return lax.div(u, p.chunks), lax.rem(u, p.chunks)

    def tick(t, carry):
        g, j = place_of(t)

        @pl.when(t < p.units)
        def _():
            @pl.when(j == 0)
            def _():
                gather_rest(g)

            forward(t, g, j)

        @pl.when((t < p.units) & (j == 1))
        def _():
            @pl.when(g + 1 < p.groups)
            def _():
                gather_pass(g + 1)

            turned[:, pl.ds(pl.multiple_of(g * p.rows, 128), p.rows)] = toks[g].T

        for lag, stage in ((LAG_SUM, activate), (LAG_PASS, hand_on), (LAG_BACK, backward)):
            u = t - lag

            @pl.when((u >= 0) & (u < p.units))
            def _(u=u, stage=stage):
                stage(u, *place_of(u))

        @pl.when(t < p.units)
        def _():
            pair_sum(t)

        u = t - LAG_BACK - 2

        @pl.when((u >= 0) & (lax.rem(u + p.chunks, p.chunks) == p.chunks - 1))
        def _():
            for h in range(p.halves):
                reduce_pair(lax.div(u, p.chunks), h)

        return carry

    lax.fori_loop(0, p.units + LAG_BACK, tick, 0)

    save_turned = pltpu.make_async_copy(turned, turned_out, local_sem.at[0])
    save_grads = pltpu.make_async_copy(grads, grads_out, local_sem.at[1])
    save_turned.start()
    save_grads.start()
    last = p.groups - 1
    for g in range(last):
        for h in range(p.halves):
            reduce_line(g, h)
    for h in range(p.halves):
        reduce_pair(last, h)
    for h in range(p.halves):
        reduce_line(last, h)
    save_in = pltpu.make_async_copy(inout, ingrad, local_sem.at[2])
    save_in.start()

    def drain(u, carry):
        g, j = place_of(u)
        c1_copy(u).wait_send()
        for step in range(1, p.chips):
            c2_copy(u, step).wait_send()
            c3_copy(u, g, j, step).wait_send()
        for step in range(p.chips):
            c4_copy(u, g, j, step).wait_send()
        for i in range(p.per_owner):
            hid_copy(u, g, j, i).wait()
        return carry

    lax.fori_loop(0, p.units, drain, 0)
    for g in range(p.groups):
        ag_pair(g).wait_send()
        for step in range(1, p.line):
            ag_line(g, step).wait_send()
            ag_pass(g, step).wait_send()
        for h in range(p.halves):
            r1_copy(g, h).wait_send()
            for step in range(1, p.line):
                r2_copy(g, h, step).wait_send()
    save_mask.wait()
    save_turned.wait()
    save_grads.wait()
    save_in.wait()


def communicate(p, tokens, weight, tile_rows, tile_cols, count, cot):
    half = p.rows // 2
    owned = cot.shape[0]
    dma = pltpu.SemaphoreType.DMA
    tokens_all = p.groups * p.rows
    anywhere = pl.BlockSpec(memory_space=pl.ANY)
    vmem = pl.BlockSpec(memory_space=pltpu.VMEM)
    out = lambda *shape: jax.ShapeDtypeStruct(shape, BF16)
    return pl.pallas_call(
        functools.partial(comm_kernel, p),
        in_specs=[
            anywhere, anywhere, vmem, vmem, pl.BlockSpec(memory_space=pltpu.SMEM), anywhere
        ],
        out_specs=[anywhere] * 5,
        out_shape=[
            out(owned, p.wide),
            out(p.block, p.depth),
            out(p.depth, tokens_all),
            out(p.chunks, tokens_all, p.cut),
            out(p.chunks, p.row_blocks * SUB, p.cut),
        ],
        scratch_shapes=[
            pltpu.VMEM((p.chunks, p.depth, p.cut), BF16),
            pltpu.VMEM((p.chunks, p.row_blocks * SUB, p.cut), BF16),
            pltpu.VMEM((p.groups, p.rows, p.depth), BF16),
            pltpu.VMEM((p.depth, tokens_all), BF16),
            pltpu.VMEM((p.chunks, tokens_all, p.cut), BF16),
            pltpu.VMEM((p.rows, p.depth), F32),
            pltpu.VMEM((p.units, half, p.cut), BF16),
            pltpu.VMEM((p.units, half, p.cut), BF16),
            pltpu.VMEM((half, p.cut), F32),
            pltpu.VMEM((p.units, p.chips, p.slab, p.cut), BF16),
            pltpu.VMEM((p.units, p.chips, p.slab, p.cut), BF16),
            pltpu.VMEM((LAG_SUM + 1, p.slab, p.cut), F32),
            pltpu.VMEM((p.units, p.slab, p.cut), BF16),
            pltpu.VMEM((owned, p.wide), BF16),
            pltpu.VMEM((p.groups, p.halves, p.line * SUB, p.part), BF16),
            pltpu.VMEM((p.groups, p.halves, p.line * SUB, p.part), BF16),
            pltpu.VMEM((p.groups, p.halves, p.line * SUB, p.part), F32),
            pltpu.VMEM((p.groups, p.halves, p.line, SUB, p.part), BF16),
            pltpu.VMEM((p.groups, p.halves, p.line, SUB, p.part), BF16),
            pltpu.VMEM((p.groups, p.halves, SUB, p.part), F32),
            pltpu.VMEM((p.block, p.depth), BF16),
            dma((p.chunks,)),
            dma((p.groups + 2,)),
            dma((p.units, p.per_owner)),
            dma((p.groups, p.line)),
            dma((p.groups, p.line)),
            dma((p.groups, p.n_row)),
            dma((p.units,)),
            dma((p.units,)),
            dma((p.units, p.chips)),
            dma((p.units, p.chips)),
            dma((p.units, p.chips)),
            dma((p.units, p.chips)),
            dma((p.units, p.chips)),
            dma((p.units, p.chips)),
            dma((p.groups, p.halves)),
            dma((p.groups, p.halves)),
            dma((p.groups, p.halves, p.line)),
            dma((p.groups, p.halves, p.line)),
        ],
        compiler_params=pltpu.CompilerParams(
            collective_id=0, has_side_effects=True, vmem_limit_bytes=60 * 1024 * 1024
        ),
        name="exchange",
    )(tokens, weight, tile_rows, tile_cols, count, cot)


def weight_kernel(p, turned, grads, mask, hidden_in, ingrad_in, weight_grad, hidden, ingrad):
    hidden[...] = hidden_in[...]
    ingrad[...] = ingrad_in[...]
    for block in range(p.row_blocks):
        rows = pl.ds(block * TILE, TILE)
        product = jnp.dot(turned[rows, :], grads[0], preferred_element_type=F32)
        one = mask[0, pl.ds(block * SUB, SUB), :]
        keep = jnp.concatenate([one] * (TILE // SUB), axis=0)
        weight_grad[rows, :] = product.astype(BF16) * keep


def finish(p, turned, grads, mask, hidden, ingrad):
    width = min(512, p.cut)
    per = p.cut // width
    owned = hidden.shape[0]
    chunked = lambda a: pl.BlockSpec((1, a.shape[1], width), lambda i: (i // per, 0, i % per))
    column = lambda rows: pl.BlockSpec((rows, width), lambda i: (0, i))
    whole = lambda a: pl.BlockSpec(a.shape, lambda i: (0,) * a.ndim)
    shape = jax.ShapeDtypeStruct
    return pl.pallas_call(
        functools.partial(weight_kernel, p),
        grid=(p.wide // width,),
        in_specs=[whole(turned), chunked(grads), chunked(mask), column(owned), whole(ingrad)],
        out_specs=[column(p.depth), column(owned), whole(ingrad)],
        out_shape=[
            shape((p.depth, p.wide), BF16), shape(hidden.shape, BF16), shape(ingrad.shape, BF16)
        ],
        compiler_params=pltpu.CompilerParams(
            dimension_semantics=("arbitrary",), vmem_limit_bytes=48 * 1024 * 1024
        ),
        name="weight_grad",
    )(turned, grads, mask, hidden, ingrad)


def on_device(n_row, n_col, tokens, weight, tile_rows, tile_cols, tile_count, cot):
    p = Plan(n_row, n_col, tokens, weight)
    hidden, ingrad, turned, grads, mask = communicate(
        p, tokens, weight, tile_rows, tile_cols, tile_count, cot
    )
    weight_grad, hidden, ingrad = finish(p, turned, grads, mask, hidden, ingrad)
    return hidden, ingrad, weight_grad


def solution(mesh):
    in_specs = (
        P("row", "col"),
        P("col", "row"),
        P("row", "col", None),
        P("row", "col", None),
        P("row", "col"),
        P("col", "row"),
    )
    out_specs = (P("col", "row"), P("row", "col"), P("col", "row"))
    return jax.shard_map(
        functools.partial(on_device, mesh.shape["row"], mesh.shape["col"]),
        mesh=mesh, in_specs=in_specs, out_specs=out_specs, check_vma=False,
    )
```

time: 197 us -> 97 us (0.49)
  waiting for transfers between devices: 119 us -> 0 us
  Pallas kernels: 38 us -> 90.3 us
  between operations: 14.8 us -> 1.3 us
  other arithmetic: 9.56 us -> 0 us
  starting transfers between devices: 7.19 us -> 0 us
  local copies, waits for them, and re-layouts: 7.3 us -> 5.05 us
    all_gather x2 -> x0, waiting for transfers between devices: 73.3 us -> none  [the longest x1 46.3 us: on_device(): full_tokens = lax.all_gather(tokens, 'row', axis=0, tiled=True)]
    pallas_call x3 -> x2, Pallas kernels: 38 us -> 90.3 us  [the longest x1 77.4 us: communicate(): pl.pallas_call(functools.partial(comm_kernel, p), in_specs=[anywhere, any...]
    all_to_all x1 -> x0, waiting for transfers between devices: 23 us -> none  [exchange_sum(): lax.all_to_all(partial.reshape(n, rows, partial.shape[1]), axis, split_ax...]
    ppermute x2 -> x0, waiting for transfers between devices: 22.2 us -> none  [the longest x1 18.4 us: paired_exchange_sum(): lax.ppermute(pair_block((chip + step) % chips).astype(jnp.bfloat16), axis...]
    convert_element_type x2 -> x0, other arithmetic: 5.81 us -> none  [the longest x1 3.62 us: on_device(): (hidden_cotangent.astype(jnp.float32) * silu_slope).astype(jnp.bfloat16)]
    all_to_all x1 -> x0, starting transfers between devices: 5.65 us -> none  [exchange_sum(): lax.all_to_all(partial.reshape(n, rows, partial.shape[1]), axis, split_ax...]
    reduce_sum x1 -> x0, other arithmetic: 2.37 us -> none  [exchange_sum(): return mine.astype(jnp.float32).sum(axis=0)]
  transfers between devices with their start and end apart: 5 -> 0, of which waited for: 5 -> 0; matrix products, arithmetic and copies ran while one was open for 2% -> 0% of each run, Pallas kernels for 6% -> 0%
where the time goes in v1:
time: 97 us; the launch traced here: 96.6 us
  Pallas kernels  90.3 us (93%)
  local copies, waits for them, and re-layouts  5.05 us (5%)
  between operations  1.3 us (1%)
    pallas_call x1, Pallas kernels, communicate(): pl.pallas_call(functools.partial(comm_kernel, p), in_specs=[anywhere, any...  77.4 us
    pallas_call x1, Pallas kernels, finish(): pl.pallas_call(functools.partial(weight_kernel, p), grid=(p.wide // width...  12.9 us
    unnamed x8, local copies, waits for them, and re-layouts  5.05 us

profile of v1, /device:TPU:0, one launch (start us, length us, event | category | flops | bytes accessed | tf_op | source)
XLA Modules:
  0.0 96.6 jit_solution(6680641109121695121)
XLA Ops:
  1.3 77.4 %exchange.1 = (bf16[96,4096]{1,0:T(8,128)(2,1)}, bf16[48,2048]{1,0:T(8,128)(2,1)}, bf16[2048,384]{1,0:T(8,128)(2,1)}, bf16[4,384,1024]{2,1,0:T(8,128)(2,1)}, bf16[4,256,1024]{2,1,0:T(8,128)(2,1)}) custom-call(bf16[48,2048]{1,0:T(8,128)(2,1)} %tokens.1, bf16[2048,4096]{1,0:T(8,128)(2,1)} %weight.1, s32[1,1,256]{2,1,0:T(1,128)} %tile_rows.1, ...), custom_call_target="tpu_custom_call" | custom-call | tf_op jit(solution)/shard_map/exchange/pallas_call | solution.py:415
  78.7 0.0 copy-start
  78.7 1.6 %copy-done = bf16[4,256,1024]{2,1,0:T(8,128)(2,1)S(1)} copy-done((bf16[4,256,1024]{2,1,0:T(8,128)(2,1)S(1)}, bf16[4,256,1024]{2,1,0:T(8,128)(2,1)}, u32[]{:S(2)}) %copy-start) | copy-done | bytes 2097176
  80.3 0.0 copy-start.1
  80.3 1.4 %copy-done.1 = bf16[2048,384]{1,0:T(8,128)(2,1)S(1)} copy-done((bf16[2048,384]{1,0:T(8,128)(2,1)S(1)}, bf16[2048,384]{1,0:T(8,128)(2,1)}, u32[]{:S(2)}) %copy-start.1) | copy-done | bytes 1572888
  81.7 0.0 copy-start.2
  81.7 1.1 %copy-done.2 = bf16[96,4096]{1,0:T(8,128)(2,1)S(1)} copy-done((bf16[96,4096]{1,0:T(8,128)(2,1)S(1)}, bf16[96,4096]{1,0:T(8,128)(2,1)}, u32[]{:S(2)}) %copy-start.2) | copy-done | bytes 786456
  82.8 0.0 copy-start.3
  82.8 0.9 copy-done.3
  83.8 12.9 %weight_grad.1 = (bf16[2048,4096]{1,0:T(8,128)(2,1)}, bf16[96,4096]{1,0:T(8,128)(2,1)}, bf16[48,2048]{1,0:T(8,128)(2,1)}) custom-call(bf16[2048,384]{1,0:T(8,128)(2,1)S(1)} %copy-done.1, bf16[4,384,1024]{2,1,0:T(8,128)(2,1)} %get-tuple-element.12.grads, bf16[4,256,1024]{2,1,0:T(8,128)(2,1)S(1)} %copy-done, bf16[96,4096]{1,0:T(8,128)(2,1)S(1)} %copy-done.2, ...), custom_call_target="tpu_custom_call" | custom-call | tf_op jit(solution)/shard_map/weight_grad/pallas_call | solution.py:495
Async XLA Ops:
  78.7 1.6 %copy-start = (bf16[4,256,1024]{2,1,0:T(8,128)(2,1)S(1)}, bf16[4,256,1024]{2,1,0:T(8,128)(2,1)}, u32[]{:S(2)}) copy-start(bf16[4,256,1024]{2,1,0:T(8,128)(2,1)} %get-tuple-element.13.mask) | copy-start | bytes 6291460
  80.3 1.4 %copy-start.1 = (bf16[2048,384]{1,0:T(8,128)(2,1)S(1)}, bf16[2048,384]{1,0:T(8,128)(2,1)}, u32[]{:S(2)}) copy-start(bf16[2048,384]{1,0:T(8,128)(2,1)} %get-tuple-element.11.turned) | copy-start | bytes 4718596
  81.7 1.1 %copy-start.2 = (bf16[96,4096]{1,0:T(8,128)(2,1)S(1)}, bf16[96,4096]{1,0:T(8,128)(2,1)}, u32[]{:S(2)}) copy-start(bf16[96,4096]{1,0:T(8,128)(2,1)} %get-tuple-element.14.hidden_in) | copy-start | bytes 2359300
  82.8 0.9 copy-start.3

commit v2 on v1

--- a/solution.py
+++ b/solution.py
@@ -32,6 +32,8 @@
         self.cut = self.wide // self.chunks
         self.units = self.groups * self.chunks
         self.halves = 2
+        self.pieces = 2
+        self.strip = self.depth // self.pieces
         self.part = self.depth // self.halves
         self.step = min(256, self.cut)
         self.row_blocks = self.depth // TILE
@@ -86,28 +88,36 @@
     def load_own(g):
         return pltpu.make_async_copy(own_rows(g), tok_rows(g, row), local_sem.at[g])
 
-    def ag_line(g, step):
-        return remote(
-            own_rows(g), tok_rows(g, row), ag_send.at[g, step], ag_recv.at[g, row],
-            (line_peer(step) * 2 + pair, col),
-        )
-
-    def ag_pair(g):
-        return remote(
-            own_rows(g), tok_rows(g, row), ag_send.at[g, 0], ag_recv.at[g, row], partner
-        )
-
-    def ag_pass(g, step):
+    def own_piece(g, q):
+        rows = pl.ds(pl.multiple_of(g * SUB, SUB), SUB)
+        return tokens.at[rows, pl.ds(q * p.strip, p.strip)]
+
+    def tok_piece(g, q, block):
+        return toks.at[g, pl.ds(place(block), SUB), pl.ds(q * p.strip, p.strip)]
+
+    def ag_line(g, q, step):
+        return remote(
+            own_piece(g, q), tok_piece(g, q, row), ag_send.at[g, q, step],
+            ag_recv.at[g, q, row], (line_peer(step) * 2 + pair, col),
+        )
+
+    def ag_pair(g, q):
+        return remote(
+            own_piece(g, q), tok_piece(g, q, row), ag_send.at[g, q, 0],
+            ag_recv.at[g, q, row], partner,
+        )
+
+    def ag_pass(g, q, step):
         block = line_peer(step) * 2 + pair
         return remote(
-            tok_rows(g, block), tok_rows(g, block), ag_fwd.at[g, step], ag_recv.at[g, block],
-            partner,
-        )
-
-    def ag_arrival(g, block):
-        return remote(
-            tok_rows(g, block), tok_rows(g, block), ag_send.at[g, 0], ag_recv.at[g, block],
-            partner,
+            tok_piece(g, q, block), tok_piece(g, q, block), ag_fwd.at[g, q, step],
+            ag_recv.at[g, q, block], partner,
+        )
+
+    def ag_arrival(g, q, block):
+        return remote(
+            tok_piece(g, q, block), tok_piece(g, q, block), ag_send.at[g, q, 0],
+            ag_recv.at[g, q, block], partner,
         )
 
     def slab_rows(j, g, index):
@@ -163,19 +173,21 @@
         )
 
     def gather_start(g):
-        for step in range(1, p.line):
-            ag_line(g, step).start()
-        ag_pair(g).start()
+        for q in range(p.pieces):
+            for step in range(1, p.line):
+                ag_line(g, q, step).start()
+            ag_pair(g, q).start()
 
     def gather_pass(g):
-        for step in range(1, p.line):
-            block = line_peer(step) * 2 + pair
-            ag_arrival(g, block).wait_recv()
-            ag_pass(g, step).start()
+        for q in range(p.pieces):
+            for step in reversed(range(1, p.line)):
+                ag_arrival(g, q, line_peer(step) * 2 + pair).wait_recv()
+                ag_pass(g, q, step).start()
 
     def gather_rest(g):
-        for step in range(p.line):
-            ag_arrival(g, line_peer(step) * 2 + 1 - pair).wait_recv()
+        for q in range(p.pieces):
+            for step in range(p.line):
+                ag_arrival(g, q, line_peer(step) * 2 + 1 - pair).wait_recv()
 
     def mask_chunk(j):
         load_weight(j).wait()
@@ -189,7 +201,7 @@
         for n in range(p.cut // p.step):
             cols = pl.ds(n * p.step, p.step)
             product = jnp.dot(toks[g], w[j, :, cols], preferred_element_type=F32)
-            keep[:, cols] = product[:half]
+            keep[lax.rem(u, 2), :, cols] = product[:half]
             c1s[u, :, cols] = product[half:].astype(BF16)
         c1_copy(u).start()
 
@@ -197,10 +209,10 @@
         c1_copy(u).wait_recv()
         for step in range(1, p.chips):
             rows = pl.ds(pl.multiple_of(chip_peer(step) * p.slab, SUB), p.slab)
-            c2s[u, step] = (keep[rows, :] + c1r[u, rows, :].astype(F32)).astype(BF16)
+            c2s[u, step] = (keep[lax.rem(u, 2), rows, :] + c1r[u, rows, :].astype(F32)).astype(BF16)
             c2_copy(u, step).start()
         rows = pl.ds(pl.multiple_of(chip * p.slab, SUB), p.slab)
-        own[lax.rem(u, LAG_SUM + 1)] = keep[rows, :] + c1r[u, rows, :].astype(F32)
+        own[lax.rem(u, LAG_SUM + 1)] = keep[lax.rem(u, 2), rows, :] + c1r[u, rows, :].astype(F32)
 
     def activate(u, g, j):
         for step in range(1, p.chips):
@@ -232,18 +244,29 @@
     def backward(u, g, j):
         for step in range(p.chips):
             c4_copy(u, g, j, step).wait_recv()
-        first = (j == 0).astype(F32)
         left = grads[j, pl.ds(pl.multiple_of(g * p.rows, SUB), p.rows), :]
-        for h in range(p.halves):
-            for n in range(p.part // p.step):
-                cols = pl.ds(h * p.part + n * p.step, p.step)
-                product = lax.dot_general(
-                    left, w[j, cols, :], (((1,), (1,)), ((), ())), preferred_element_type=F32
-                )
-                share[:, cols] = jnp.where(first > 0.5, 0.0, share[:, cols]) + product
-
-            @pl.when(j == p.chunks - 1)
-            def _():
+
+        def product(start):
+            return lax.dot_general(
+                left, w[j, pl.ds(start, TILE), :], (((1,), (1,)), ((), ())),
+                preferred_element_type=F32,
+            )
+
+        @pl.when(j == 0)
+        def _():
+            for start in range(0, p.depth, TILE):
+                share[:, pl.ds(start, TILE)] = product(start)
+
+        @pl.when((j > 0) & (j < p.chunks - 1))
+        def _():
+            for start in range(0, p.depth, TILE):
+                share[:, pl.ds(start, TILE)] += product(start)
+
+        @pl.when(j == p.chunks - 1)
+        def _():
+            for h in range(p.halves):
+                for start in range(h * p.part, (h + 1) * p.part, TILE):
+                    share[:, pl.ds(start, TILE)] += product(start)
                 cols = pl.ds(h * p.part, p.part)
                 for k in range(p.line):
                     away = share[pl.ds(place(2 * k + 1 - pair), SUB), cols]
@@ -289,7 +312,7 @@
     cap = tile_rows.shape[2]
     local_rows = tile_rows[0] - col * p.row_blocks
     local_cols = tile_cols[0] - row * p.col_blocks
-    live = lax.broadcasted_iota(jnp.int32, (1, cap), 1) < count[0, 0]
+    live = lax.broadcasted_iota(jnp.int32, (1, cap), 1) < count[...]
     local_rows = jnp.where(live, local_rows, -1)
     row_of = lax.broadcasted_iota(jnp.int32, (p.row_blocks * SUB, cap), 0) // SUB
     row_pick = (row_of == local_rows).astype(F32)
@@ -305,14 +328,10 @@
         mask[j] = jnp.dot(blocks, spread, preferred_element_type=F32).astype(BF16)
     save_mask = pltpu.make_async_copy(mask, mask_out, local_sem.at[p.groups + 1])
     save_mask.start()
-    early = p.chunks // 2
-    for j in range(early):
-        mask_chunk(j)
+    mask_chunk(0)
     gather_pass(0)
     for g in range(1, p.groups):
         gather_start(g)
-    for j in range(early, p.chunks):
-        mask_chunk(j)
     for g in range(p.groups):
         load_own(g).wait()
     load_cot.wait()
@@ -329,28 +348,33 @@
             def _():
                 gather_rest(g)
 
+            @pl.when((g == 0) & (j > 0))
+            def _():
+                mask_chunk(j)
+
             forward(t, g, j)
 
         @pl.when((t < p.units) & (j == 1))
         def _():
-            @pl.when(g + 1 < p.groups)
+            turned[:, pl.ds(pl.multiple_of(g * p.rows, 128), p.rows)] = toks[g].T
+
+        def late(lag, stage):
+            u = t - lag
+
+            @pl.when((u >= 0) & (u < p.units))
             def _():
-                gather_pass(g + 1)
-
-            turned[:, pl.ds(pl.multiple_of(g * p.rows, 128), p.rows)] = toks[g].T
-
-        for lag, stage in ((LAG_SUM, activate), (LAG_PASS, hand_on), (LAG_BACK, backward)):
-            u = t - lag
-
-            @pl.when((u >= 0) & (u < p.units))
-            def _(u=u, stage=stage):
                 stage(u, *place_of(u))
 
-        @pl.when(t < p.units)
-        def _():
-            pair_sum(t)
-
-        u = t - LAG_BACK - 2
+        late(1, lambda u, g, j: pair_sum(u))
+        late(LAG_PASS, hand_on)
+        late(LAG_BACK, backward)
+        late(LAG_SUM, activate)
+
+        @pl.when((j == 1) & (g + 1 < p.groups))
+        def _():
+            gather_pass(g + 1)
+
+        u = t - LAG_BACK - 3
 
         @pl.when((u >= 0) & (lax.rem(u + p.chunks, p.chunks) == p.chunks - 1))
         def _():
@@ -359,20 +383,44 @@
 
         return carry
 
-    lax.fori_loop(0, p.units + LAG_BACK, tick, 0)
+    lax.fori_loop(0, p.units, tick, 0)
+
+    pair_sum(p.units - 1)
+    for u in range(p.units - LAG_SUM, p.units - 1):
+        activate(u, *divmod(u, p.chunks))
+
+    def tail(i, carry):
+        @pl.when(i < LAG_PASS)
+        def _():
+            u = p.units - LAG_PASS + i
+            hand_on(u, *place_of(u))
+
+        @pl.when(i == p.chunks)
+        def _():
+            for h in range(p.halves):
+                reduce_pair(p.groups - 2, h)
+
+        u = p.units - LAG_BACK + i
+        backward(u, *place_of(u))
+
+        @pl.when(i == 1)
+        def _():
+            activate(p.units - 1, *divmod(p.units - 1, p.chunks))
+
+        return carry
+
+    lax.fori_loop(0, LAG_BACK, tail, 0)
 
     save_turned = pltpu.make_async_copy(turned, turned_out, local_sem.at[0])
     save_grads = pltpu.make_async_copy(grads, grads_out, local_sem.at[1])
     save_turned.start()
     save_grads.start()
     last = p.groups - 1
-    for g in range(last):
+    for h in range(p.halves):
+        reduce_pair(last, h)
+    for g in range(p.groups):
         for h in range(p.halves):
             reduce_line(g, h)
-    for h in range(p.halves):
-        reduce_pair(last, h)
-    for h in range(p.halves):
-        reduce_line(last, h)
     save_in = pltpu.make_async_copy(inout, ingrad, local_sem.at[2])
     save_in.start()
 
@@ -390,10 +438,11 @@
 
     lax.fori_loop(0, p.units, drain, 0)
     for g in range(p.groups):
-        ag_pair(g).wait_send()
-        for step in range(1, p.line):
-            ag_line(g, step).wait_send()
-            ag_pass(g, step).wait_send()
+        for q in range(p.pieces):
+            ag_pair(g, q).wait_send()
+            for step in range(1, p.line):
+                ag_line(g, q, step).wait_send()
+                ag_pass(g, q, step).wait_send()
         for h in range(p.halves):
             r1_copy(g, h).wait_send()
             for step in range(1, p.line):
@@ -415,7 +464,7 @@
     return pl.pallas_call(
         functools.partial(comm_kernel, p),
         in_specs=[
-            anywhere, anywhere, vmem, vmem, pl.BlockSpec(memory_space=pltpu.SMEM), anywhere
+            anywhere, anywhere, vmem, vmem, vmem, anywhere
         ],
         out_specs=[anywhere] * 5,
         out_shape=[
@@ -434,7 +483,7 @@
             pltpu.VMEM((p.rows, p.depth), F32),
             pltpu.VMEM((p.units, half, p.cut), BF16),
             pltpu.VMEM((p.units, half, p.cut), BF16),
-            pltpu.VMEM((half, p.cut), F32),
+            pltpu.VMEM((2, half, p.cut), F32),
             pltpu.VMEM((p.units, p.chips, p.slab, p.cut), BF16),
             pltpu.VMEM((p.units, p.chips, p.slab, p.cut), BF16),
             pltpu.VMEM((LAG_SUM + 1, p.slab, p.cut), F32),
@@ -450,9 +499,9 @@
             dma((p.chunks,)),
             dma((p.groups + 2,)),
             dma((p.units, p.per_owner)),
-            dma((p.groups, p.line)),
-            dma((p.groups, p.line)),
-            dma((p.groups, p.n_row)),
+            dma((p.groups, p.pieces, p.line)),
+            dma((p.groups, p.pieces, p.line)),
+            dma((p.groups, p.pieces, p.n_row)),
             dma((p.units,)),
             dma((p.units,)),
             dma((p.units, p.chips)),
@@ -485,7 +534,7 @@
 
 
 def finish(p, turned, grads, mask, hidden, ingrad):
-    width = min(512, p.cut)
+    width = min(1024, p.cut)
     per = p.cut // width
     owned = hidden.shape[0]
     chunked = lambda a: pl.BlockSpec((1, a.shape[1], width), lambda i: (i // per, 0, i % per))
@@ -501,7 +550,7 @@
             shape((p.depth, p.wide), BF16), shape(hidden.shape, BF16), shape(ingrad.shape, BF16)
         ],
         compiler_params=pltpu.CompilerParams(
-            dimension_semantics=("arbitrary",), vmem_limit_bytes=48 * 1024 * 1024
+            dimension_semantics=("arbitrary",), vmem_limit_bytes=62 * 1024 * 1024
         ),
         name="weight_grad",
     )(turned, grads, mask, hidden, ingrad)

time: 97 us -> 91.9 us (0.947)
  local copies, waits for them, and re-layouts: 5.05 us -> 0 us
    unnamed x8 -> x0, local copies, waits for them, and re-layouts: 5.05 us -> none
where the time goes in v2:
time: 91.9 us; the launch traced here: 91.7 us
  Pallas kernels  90.4 us (98%)
  between operations  1.29 us (1%)
    pallas_call x1, Pallas kernels, communicate(): pl.pallas_call(functools.partial(comm_kernel, p), in_specs=[anywhere, any...  76.6 us
    pallas_call x1, Pallas kernels, finish(): pl.pallas_call(functools.partial(weight_kernel, p), grid=(p.wide // width...  13.7 us

profile of v2, /device:TPU:0, one launch (start us, length us, event | category | flops | bytes accessed | tf_op | source)
XLA Modules:
  0.0 91.7 jit_solution(14759656863211300361)
XLA Ops:
  1.3 76.6 %exchange.1 = (bf16[96,4096]{1,0:T(8,128)(2,1)}, bf16[48,2048]{1,0:T(8,128)(2,1)}, bf16[2048,384]{1,0:T(8,128)(2,1)}, bf16[4,384,1024]{2,1,0:T(8,128)(2,1)}, bf16[4,256,1024]{2,1,0:T(8,128)(2,1)}) custom-call(bf16[48,2048]{1,0:T(8,128)(2,1)} %tokens.1, bf16[2048,4096]{1,0:T(8,128)(2,1)} %weight.1, s32[1,1,256]{2,1,0:T(1,128)} %tile_rows.1, ...), custom_call_target="tpu_custom_call" | custom-call | tf_op jit(solution)/shard_map/exchange/pallas_call | solution.py:464
  77.9 13.7 %weight_grad.1 = (bf16[2048,4096]{1,0:T(8,128)(2,1)}, bf16[96,4096]{1,0:T(8,128)(2,1)}, bf16[48,2048]{1,0:T(8,128)(2,1)}) custom-call(bf16[2048,384]{1,0:T(8,128)(2,1)} %get-tuple-element.11.turned, bf16[4,384,1024]{2,1,0:T(8,128)(2,1)} %get-tuple-element.12.grads, bf16[4,256,1024]{2,1,0:T(8,128)(2,1)} %get-tuple-element.13.mask, ...), custom_call_target="tpu_custom_call" | custom-call | tf_op jit(solution)/shard_map/weight_grad/pallas_call | solution.py:544

commit v3 on v2

--- a/solution.py
+++ b/solution.py
@@ -40,13 +40,27 @@
         self.col_blocks = self.wide // TILE
 
 
+def weight_rows(turned, grads, mask, target, block):
+    rows = pl.ds(pl.multiple_of(block * TILE, TILE), TILE)
+    one = mask[pl.ds(pl.multiple_of(block * SUB, SUB), SUB), :]
+    keep = jnp.concatenate([one] * (TILE // SUB), axis=0)
+    wide = target.shape[1]
+    step = min(512, wide)
+    for start in range(0, wide, step):
+        cols = slice(start, start + step)
+        product = jnp.dot(
+            turned[rows, :], grads[:, pl.ds(start, step)], preferred_element_type=F32
+        )
+        target[rows, pl.ds(start, step)] = product.astype(BF16) * keep[:, cols]
+
+
 def comm_kernel(
     p,
-    tokens, weight, tile_rows, tile_cols, count, cot,
-    hidden, ingrad, turned_out, grads_out, mask_out,
+    tokens, weight, rows_in, cols_in, count_in, cot,
+    hidden, ingrad, turned_out, grads_out, mask_out, first_out,
     w, mask, toks, turned, grads, share, c1s, c1r, keep, c2s, c2r, own, hid, cotv,
-    r1s, r1r, rkeep, r2s, r2r, rown, inout,
-    w_sem, local_sem, hid_sem,
+    r1s, r1r, rkeep, r2s, r2r, rown, inout, tile_rows, tile_cols, count,
+    w_sem, local_sem, hid_sem, index_sem,
     ag_send, ag_fwd, ag_recv, c1_send, c1_recv, c2_send, c2_recv, c3_send, c3_recv,
     c4_send, c4_recv, r1_send, r1_recv, r2_send, r2_recv,
 ):
@@ -271,7 +285,13 @@
                 for k in range(p.line):
                     away = share[pl.ds(place(2 * k + 1 - pair), SUB), cols]
                     r1s[g, h, k * SUB : (k + 1) * SUB, :] = away.astype(BF16)
-                r1_copy(g, h).start()
+                if h:
+
+                    @pl.when(g < p.groups - 1)
+                    def _():
+                        r1_copy(g, h).start()
+                else:
+                    r1_copy(g, h).start()
                 for k in range(p.line):
                     stay = share[pl.ds(place(2 * k + pair), SUB), cols]
                     rkeep[g, h, k * SUB : (k + 1) * SUB, :] = stay
@@ -286,6 +306,14 @@
         rows = pl.ds(pl.multiple_of(line * SUB, SUB), SUB)
         rown[g, h] = rkeep[g, h, rows, :] + r1r[g, h, rows, :].astype(F32)
 
+    def first_chunk(part):
+        def one_block(block, carry):
+            weight_rows(turned, grads.at[0], mask.at[0], w.at[0], block)
+            return carry
+
+        each = p.row_blocks // 4
+        lax.fori_loop(part * each, (part + 1) * each, one_block, 0)
+
     def reduce_line(g, h):
         total = rown[g, h]
         for step in range(1, p.line):
@@ -293,6 +321,14 @@
             total = total + r2r[g, h, step].astype(F32)
         inout[g * SUB : (g + 1) * SUB, h * p.part : (h + 1) * p.part] = total.astype(BF16)
 
+    index_loads = [
+        pltpu.make_async_copy(source, target, index_sem.at[i])
+        for i, (source, target) in enumerate(
+            ((rows_in, tile_rows), (cols_in, tile_cols), (count_in, count))
+        )
+    ]
+    for load in index_loads:
+        load.start()
     for j in range(p.chunks):
         load_weight(j).start()
     load_cot = pltpu.make_async_copy(cot, cotv, local_sem.at[p.groups])
@@ -309,6 +345,8 @@
     pl.semaphore_wait(barrier, len(peers))
     gather_start(0)
 
+    for load in index_loads:
+        load.wait()
     cap = tile_rows.shape[2]
     local_rows = tile_rows[0] - col * p.row_blocks
     local_cols = tile_cols[0] - row * p.col_blocks
@@ -330,8 +368,7 @@
     save_mask.start()
     mask_chunk(0)
     gather_pass(0)
-    for g in range(1, p.groups):
-        gather_start(g)
+    gather_start(1)
     for g in range(p.groups):
         load_own(g).wait()
     load_cot.wait()
@@ -373,6 +410,10 @@
         @pl.when((j == 1) & (g + 1 < p.groups))
         def _():
             gather_pass(g + 1)
+
+            @pl.when(g + 2 < p.groups)
+            def _():
+                gather_start(g + 2)
 
         u = t - LAG_BACK - 3
 
@@ -416,8 +457,16 @@
     save_turned.start()
     save_grads.start()
     last = p.groups - 1
-    for h in range(p.halves):
-        reduce_pair(last, h)
+    save_first = pltpu.make_async_copy(w.at[0], first_out, local_sem.at[3])
+    first_chunk(0)
+    first_chunk(1)
+    r1_copy(last, 0).wait_send()
+    r1_copy(last, 1).start()
+    first_chunk(2)
+    reduce_pair(last, 0)
+    first_chunk(3)
+    save_first.start()
+    reduce_pair(last, 1)
     for g in range(p.groups):
         for h in range(p.halves):
             reduce_line(g, h)
@@ -444,13 +493,15 @@
                 ag_line(g, q, step).wait_send()
                 ag_pass(g, q, step).wait_send()
         for h in range(p.halves):
-            r1_copy(g, h).wait_send()
+            if g < last or h + 1 == p.halves:
+                r1_copy(g, h).wait_send()
             for step in range(1, p.line):
                 r2_copy(g, h, step).wait_send()
     save_mask.wait()
     save_turned.wait()
     save_grads.wait()
     save_in.wait()
+    save_first.wait()
 
 
 def communicate(p, tokens, weight, tile_rows, tile_cols, count, cot):
@@ -459,20 +510,18 @@
     dma = pltpu.SemaphoreType.DMA
     tokens_all = p.groups * p.rows
     anywhere = pl.BlockSpec(memory_space=pl.ANY)
-    vmem = pl.BlockSpec(memory_space=pltpu.VMEM)
     out = lambda *shape: jax.ShapeDtypeStruct(shape, BF16)
     return pl.pallas_call(
         functools.partial(comm_kernel, p),
-        in_specs=[
-            anywhere, anywhere, vmem, vmem, vmem, anywhere
-        ],
-        out_specs=[anywhere] * 5,
+        in_specs=[anywhere] * 2 + [pl.BlockSpec(memory_space=pltpu.HBM)] * 3 + [anywhere],
+        out_specs=[anywhere] * 6,
         out_shape=[
             out(owned, p.wide),
             out(p.block, p.depth),
             out(p.depth, tokens_all),
             out(p.chunks, tokens_all, p.cut),
             out(p.chunks, p.row_blocks * SUB, p.cut),
+            out(p.depth, p.cut),
         ],
         scratch_shapes=[
             pltpu.VMEM((p.chunks, p.depth, p.cut), BF16),
@@ -496,9 +545,13 @@
             pltpu.VMEM((p.groups, p.halves, p.line, SUB, p.part), BF16),
             pltpu.VMEM((p.groups, p.halves, SUB, p.part), F32),
             pltpu.VMEM((p.block, p.depth), BF16),
+            pltpu.VMEM(tile_rows.shape, jnp.int32),
+            pltpu.VMEM(tile_cols.shape, jnp.int32),
+            pltpu.VMEM(count.shape, jnp.int32),
             dma((p.chunks,)),
             dma((p.groups + 2,)),
             dma((p.units, p.per_owner)),
+            dma((3,)),
             dma((p.groups, p.pieces, p.line)),
             dma((p.groups, p.pieces, p.line)),
             dma((p.groups, p.pieces, p.n_row)),
@@ -522,46 +575,95 @@
     )(tokens, weight, tile_rows, tile_cols, count, cot)
 
 
-def weight_kernel(p, turned, grads, mask, hidden_in, ingrad_in, weight_grad, hidden, ingrad):
-    hidden[...] = hidden_in[...]
-    ingrad[...] = ingrad_in[...]
-    for block in range(p.row_blocks):
-        rows = pl.ds(block * TILE, TILE)
-        product = jnp.dot(turned[rows, :], grads[0], preferred_element_type=F32)
-        one = mask[0, pl.ds(block * SUB, SUB), :]
-        keep = jnp.concatenate([one] * (TILE // SUB), axis=0)
-        weight_grad[rows, :] = product.astype(BF16) * keep
-
-
-def finish(p, turned, grads, mask, hidden, ingrad):
-    width = min(1024, p.cut)
-    per = p.cut // width
-    owned = hidden.shape[0]
-    chunked = lambda a: pl.BlockSpec((1, a.shape[1], width), lambda i: (i // per, 0, i % per))
-    column = lambda rows: pl.BlockSpec((rows, width), lambda i: (0, i))
-    whole = lambda a: pl.BlockSpec(a.shape, lambda i: (0,) * a.ndim)
+def weight_kernel(
+    p, turned_in, grads_in, mask_in, first_in, hidden_in, ingrad_in,
+    weight_grad, hidden, ingrad,
+    turned, grads, mask, first, stage, hid, inout, load_sem, chunk_sem, out_sem, pass_sem,
+):
+    quarter = p.depth // 4
+    blocks = p.row_blocks // 4
+
+    def load(source, target, i):
+        return pltpu.make_async_copy(source, target, load_sem.at[i])
+
+    def load_chunk(i):
+        return (
+            pltpu.make_async_copy(grads_in.at[i], grads.at[i], chunk_sem.at[i, 0]),
+            pltpu.make_async_copy(mask_in.at[i], mask.at[i], chunk_sem.at[i, 1]),
+        )
+
+    def store(i, q):
+        rows = pl.ds(q * quarter, quarter)
+        return pltpu.make_async_copy(
+            stage.at[i % 2, rows, :],
+            weight_grad.at[rows, pl.ds(i * p.cut, p.cut)],
+            out_sem.at[i % 2, q],
+        )
+
+    load_turned = load(turned_in, turned, 0)
+    loads = [
+        load(first_in, first, 1), load(hidden_in, hid, 2), load(ingrad_in, inout, 3)
+    ]
+    passes = [
+        pltpu.make_async_copy(first, weight_grad.at[:, pl.ds(0, p.cut)], pass_sem.at[0]),
+        pltpu.make_async_copy(hid, hidden, pass_sem.at[1]),
+        pltpu.make_async_copy(inout, ingrad, pass_sem.at[2]),
+    ]
+    load_turned.start()
+    for i in range(1, p.chunks):
+        for copy in load_chunk(i):
+            copy.start()
+    for copy in loads:
+        copy.start()
+    load_turned.wait()
+    for i in range(1, p.chunks):
+        for copy in load_chunk(i):
+            copy.wait()
+        for q in range(4):
+            if i > 2:
+                store(i - 2, q).wait()
+            for block in range(q * blocks, (q + 1) * blocks):
+                weight_rows(turned, grads.at[i], mask.at[i], stage.at[i % 2], block)
+            store(i, q).start()
+        if i == 1:
+            for came, sent in zip(loads, passes):
+                came.wait()
+                sent.start()
+    for i in range(max(1, p.chunks - 2), p.chunks):
+        for q in range(4):
+            store(i, q).wait()
+    for sent in passes:
+        sent.wait()
+
+
+def finish(p, turned, grads, mask, first, hidden, ingrad):
+    anywhere = pl.BlockSpec(memory_space=pl.ANY)
+    dma = pltpu.SemaphoreType.DMA
     shape = jax.ShapeDtypeStruct
+    vmem = lambda a: pltpu.VMEM(a.shape, BF16)
     return pl.pallas_call(
         functools.partial(weight_kernel, p),
-        grid=(p.wide // width,),
-        in_specs=[whole(turned), chunked(grads), chunked(mask), column(owned), whole(ingrad)],
-        out_specs=[column(p.depth), column(owned), whole(ingrad)],
+        in_specs=[anywhere] * 6,
+        out_specs=[anywhere] * 3,
         out_shape=[
             shape((p.depth, p.wide), BF16), shape(hidden.shape, BF16), shape(ingrad.shape, BF16)
         ],
-        compiler_params=pltpu.CompilerParams(
-            dimension_semantics=("arbitrary",), vmem_limit_bytes=62 * 1024 * 1024
-        ),
+        scratch_shapes=[
+            vmem(turned), vmem(grads), vmem(mask), vmem(first),
+            pltpu.VMEM((2, p.depth, p.cut), BF16), vmem(hidden), vmem(ingrad),
+            dma((4,)), dma((p.chunks, 2)), dma((2, 4)), dma((3,)),
+        ],
+        compiler_params=pltpu.CompilerParams(vmem_limit_bytes=62 * 1024 * 1024),
         name="weight_grad",
-    )(turned, grads, mask, hidden, ingrad)
+    )(turned, grads, mask, first, hidden, ingrad)
 
 
 def on_device(n_row, n_col, tokens, weight, tile_rows, tile_cols, tile_count, cot):
     p = Plan(n_row, n_col, tokens, weight)
-    hidden, ingrad, turned, grads, mask = communicate(
+    hidden, ingrad, turned, grads, mask, first = communicate(
         p, tokens, weight, tile_rows, tile_cols, tile_count, cot
     )
-    weight_grad, hidden, ingrad = finish(p, turned, grads, mask, hidden, ingrad)
+    weight_grad, hidden, ingrad = finish(p, turned, grads, mask, first, hidden, ingrad)
     return hidden, ingrad, weight_grad
 
 

time: 91.9 us -> 87.3 us (0.950)
  Pallas kernels: 90.4 us -> 85.7 us
    pallas_call x2, Pallas kernels: 90.4 us -> 85.7 us  [the longest x1 74 us: communicate(): pl.pallas_call(functools.partial(comm_kernel, p), in_specs=[anywhere] * 2...]
where the time goes in v3:
time: 87.3 us; the launch traced here: 87.2 us
  Pallas kernels  85.7 us (98%)
  between operations  1.45 us (2%)
    pallas_call x1, Pallas kernels, communicate(): pl.pallas_call(functools.partial(comm_kernel, p), in_specs=[anywhere] * 2...  74 us
    pallas_call x1, Pallas kernels, finish(): pl.pallas_call(functools.partial(weight_kernel, p), in_specs=[anywhere] *...  11.7 us

profile of v3, /device:TPU:0, one launch (start us, length us, event | category | flops | bytes accessed | tf_op | source)
XLA Modules:
  0.0 87.2 jit_solution(2444631126819413101)
XLA Ops:
  1.3 74.0 %exchange.1 = (bf16[96,4096]{1,0:T(8,128)(2,1)}, bf16[48,2048]{1,0:T(8,128)(2,1)}, bf16[2048,384]{1,0:T(8,128)(2,1)}, bf16[4,384,1024]{2,1,0:T(8,128)(2,1)}, bf1...) custom-call(bf16[48,2048]{1,0:T(8,128)(2,1)} %tokens.1, bf16[2048,4096]{1,0:T(8,128)(2,1)} %weight.1, ...), custom_call_target="tpu_custom_call" | custom-call | tf_op jit(solution)/shard_map/exchange/pallas_call | solution.py:514
  75.3 11.7 %weight_grad.1 = (bf16[2048,4096]{1,0:T(8,128)(2,1)}, bf16[96,4096]{1,0:T(8,128)(2,1)}, bf16[48,2048]{1,0:T(8,128)(2,1)}) custom-call(bf16[2048,384]{1,0:T(8,128)(2,1)} %get-tuple-element.12.turned_in, bf16[4,384,1024]{2,1,0:T(8,128)(2,1)} %get-tuple-element.13.grads_in, bf16[4,256,1024]{2,1,0:T(8,128)(2,1)} %get-tuple-element.14.mask_in, ...), custom_call_target="tpu_custom_call" | custom-call | tf_op jit(solution)/shard_map/weight_grad/pallas_call | solution.py:644

commit v4 on v3

--- a/solution.py
+++ b/solution.py
@@ -427,22 +427,27 @@
     lax.fori_loop(0, p.units, tick, 0)
 
     pair_sum(p.units - 1)
-    for u in range(p.units - LAG_SUM, p.units - 1):
-        activate(u, *divmod(u, p.chunks))
 
     def tail(i, carry):
-        @pl.when(i < LAG_PASS)
+        @pl.when((i > 0) & (i <= LAG_PASS - 1))
         def _():
             u = p.units - LAG_PASS + i
             hand_on(u, *place_of(u))
 
-        @pl.when(i == p.chunks)
+        @pl.when(i == LAG_PASS)
         def _():
             for h in range(p.halves):
                 reduce_pair(p.groups - 2, h)
 
         u = p.units - LAG_BACK + i
         backward(u, *place_of(u))
+
+        @pl.when(i == 0)
+        def _():
+            for u in range(p.units - LAG_SUM, p.units - 1):
+                activate(u, *divmod(u, p.chunks))
+            u = p.units - LAG_PASS
+            hand_on(u, *divmod(u, p.chunks))
 
         @pl.when(i == 1)
         def _():

time: 87.3 us -> 86.8 us (level)
  no operation moved by 1% of the time
where the time goes in v4:
time: 86.8 us; the launch traced here: 86.6 us
  Pallas kernels  85.2 us (98%)
  between operations  1.45 us (2%)
    pallas_call x1, Pallas kernels, communicate(): pl.pallas_call(functools.partial(comm_kernel, p), in_specs=[anywhere] * 2...  73.5 us
    pallas_call x1, Pallas kernels, finish(): pl.pallas_call(functools.partial(weight_kernel, p), in_specs=[anywhere] *...  11.7 us

profile of v4, /device:TPU:0, one launch (start us, length us, event | category | flops | bytes accessed | tf_op | source)
XLA Modules:
  0.0 86.6 jit_solution(9397916768602791413)
XLA Ops:
  1.3 73.5 %exchange.1 = (bf16[96,4096]{1,0:T(8,128)(2,1)}, bf16[48,2048]{1,0:T(8,128)(2,1)}, bf16[2048,384]{1,0:T(8,128)(2,1)}, bf16[4,384,1024]{2,1,0:T(8,128)(2,1)}, bf1...) custom-call(bf16[48,2048]{1,0:T(8,128)(2,1)} %tokens.1, bf16[2048,4096]{1,0:T(8,128)(2,1)} %weight.1, ...), custom_call_target="tpu_custom_call" | custom-call | tf_op jit(solution)/shard_map/exchange/pallas_call | solution.py:519
  74.8 11.7 %weight_grad.1 = (bf16[2048,4096]{1,0:T(8,128)(2,1)}, bf16[96,4096]{1,0:T(8,128)(2,1)}, bf16[48,2048]{1,0:T(8,128)(2,1)}) custom-call(bf16[2048,384]{1,0:T(8,128)(2,1)} %get-tuple-element.12.turned_in, bf16[4,384,1024]{2,1,0:T(8,128)(2,1)} %get-tuple-element.13.grads_in, bf16[4,256,1024]{2,1,0:T(8,128)(2,1)} %get-tuple-element.14.mask_in, ...), custom_call_target="tpu_custom_call" | custom-call | tf_op jit(solution)/shard_map/weight_grad/pallas_call | solution.py:649
